TPU v7x, 256 devices: a whole 4x4x8 slice. The times are simulated.
256 devices in a mesh: chan: 16 (over z, core), rad: 16 (over y, x).
Axes of the slice: x: 4, y: 4, z: 8, core: 2. Of those that a mesh axis runs over, the one named last changes fastest.
Arguments:
- state: float32 [2048, 2, 16, 1536], P('chan', None, None, 'rad'), may hold values from -200 to 200
- coupling: float32 [64, 16, 4, 32, 32], P('chan'), may hold values from -1.1 to 1.1
- fetch_group: int32 [16, 16], replicated, may hold values from 0 to 3
- live_slots: int32 [64], P('chan'), may hold values from 1 to 16, as said below
- radius_one: float32 [16], replicated, may hold values from 1 to 6
- radius_two: float32 [1536], P('rad'), may hold values from 1 to 6
- kinetic_diag: float32 [12, 128, 128], replicated, may hold values from -2 to 5
- kinetic_link: float32 [11, 128, 128], replicated, may hold values from -0.5 to 0.5
Outputs:
- orthogonal: float32 [2048, 2, 16, 1536], P(('chan', 'rad'))
- arnoldi_coeffs: float32 [3], replicated
Inputs may be any that keep to these rules, and one draw needn't show every extreme that they name: `live_slots`: every draw has a block with all 16 slots live.
All inputs are finite; a program needn't handle non-finite values.
Results may differ from a plain program's by a relative error of at most 0.0003.
Values sent between devices are 32-bit elements; how exact they have to be, the bound alone decides.
A program may use at most 128 MiB of HBM per device.

v0:
```python
import jax
import jax.numpy as jnp
from jax import lax
from jax.sharding import PartitionSpec as P

C = 2048
R = 1536


def radial_kernel(radius_one, radius_two, orders):
    nearer = jnp.minimum(radius_one[:, None], radius_two[None, :])
    farther = jnp.maximum(radius_one[:, None], radius_two[None, :])
    powers = jnp.arange(orders).astype(radius_one.dtype)[:, None, None]
    return nearer[None] ** powers / farther[None] ** (powers + 1.0)


def kinetic(field, kinetic_diag, kinetic_link):
    elements = kinetic_diag.shape[0]
    points = kinetic_diag.shape[1]
    rows = field.reshape(-1, elements, points)
    result = jnp.einsum("rep,eqp->req", rows, kinetic_diag, precision=lax.Precision.HIGHEST)
    lower = jnp.einsum("rep,eqp->req", rows[:, :-1], kinetic_link, precision=lax.Precision.HIGHEST)
    upper = jnp.einsum("rep,epq->req", rows[:, 1:], kinetic_link, precision=lax.Precision.HIGHEST)
    result = (
        result + jnp.pad(lower, ((0, 0), (1, 0), (0, 0))) + jnp.pad(upper, ((0, 0), (0, 1), (0, 0)))
    )
    return result.reshape(field.shape)


def coupling_products(state, coupling, fetch_group, live_slots, radius_one, radius_two):
    chan_count = lax.axis_size("chan")
    my_rank = lax.axis_index("chan")
    local_channels = state.shape[0]
    planes = state.shape[1]
    band = state.shape[2]
    radial = state.shape[3]
    groups_here = coupling.shape[0]
    orders = coupling.shape[2]
    block = coupling.shape[3]
    cells = planes * band * radial
    grouped = state.reshape(groups_here, block, cells)
    outgoing = jnp.take(grouped, fetch_group[:, my_rank], axis=0)
    incoming = lax.all_to_all(outgoing, "chan", split_axis=0, concat_axis=0, tiled=True)
    incoming = incoming.reshape(chan_count * block, cells)
    slot_of = (jnp.arange(chan_count, dtype=jnp.int32) - my_rank) % chan_count
    weights = jnp.take(coupling, slot_of, axis=1)
    active = (slot_of[None, :] < live_slots[:, None]).astype(jnp.float32)
    weights = weights * active[:, :, None, None, None]
    matrices = weights.transpose(2, 0, 3, 1, 4).reshape(orders, local_channels, chan_count * block)
    kernel = radial_kernel(radius_one, radius_two, orders)
    kernel = jnp.broadcast_to(kernel[:, None], (orders, planes, band, radial)).reshape(
        orders, cells
    )
    total = jnp.zeros((local_channels, cells), jnp.float32)
    for order in range(orders):
        product = jnp.dot(
            matrices[order],
            incoming,
            precision=lax.Precision.HIGHEST,
            preferred_element_type=jnp.float32,
        )
        total = total + kernel[order] * product
    return total.reshape(state.shape)


def per_device(
    state, coupling, fetch_group, live_slots, radius_one, radius_two, kinetic_diag, kinetic_link
):
    coupled = coupling_products(state, coupling, fetch_group, live_slots, radius_one, radius_two)
    state_here, coupled_here = (
        lax.all_to_all(state, "rad", split_axis=0, concat_axis=3, tiled=True),
        lax.all_to_all(coupled, "rad", split_axis=0, concat_axis=3, tiled=True),
    )
    applied = kinetic(state_here, kinetic_diag, kinetic_link) + coupled_here
    wave_re = applied[:, 1]
    wave_im = -applied[:, 0]
    state_re = state_here[:, 0]
    state_im = state_here[:, 1]
    total_count = 2.0 * C * state.shape[2] * R
    cross_re = jnp.sum(state_re * wave_re + state_im * wave_im)
    cross_im = jnp.sum(state_re * wave_im - state_im * wave_re)
    self_sq = jnp.sum(state_here * state_here)
    cross_re, cross_im, self_sq = lax.psum((cross_re, cross_im, self_sq), ("chan", "rad"))
    proj_re = cross_re / self_sq
    proj_im = cross_im / self_sq
    orth_re = wave_re - (proj_re * state_re - proj_im * state_im)
    orth_im = wave_im - (proj_re * state_im + proj_im * state_re)
    square_mean = (
        lax.psum(jnp.sum(orth_re * orth_re + orth_im * orth_im), ("chan", "rad")) / total_count
    )
    rms = jnp.sqrt(square_mean + 1e-06)
    orthogonal = jnp.stack([orth_re, orth_im], axis=1)
    return (orthogonal, jnp.stack([proj_re, proj_im, rms]))


def solution(mesh):
    placed = (
        P("chan", None, None, "rad"),
        P("chan", None, None, None, None),
        P(),
        P("chan"),
        P(),
        P("rad"),
        P(),
        P(),
    )
    return jax.shard_map(
        per_device,
        mesh=mesh,
        in_specs=placed,
        out_specs=(P(("chan", "rad"), None, None, None), P()),
        check_vma=False,
    )
```

profile of v0, /device:TPU:1, one launch (start us, length us, event | category | flops | bytes accessed | tf_op | source)
XLA Modules:
  0.0 410.5 jit_solution(6286049403578286027)
XLA Ops:
  2.5 3.0 copy.55
  8.0 3.6 gather_fusion.1
  11.7 6.5 %broadcast_select_fusion = f32[16,32,3072]{2,1,0:T(8,128)} fusion(f32[16,32,3072]{2,1,0:T(8,128)} %gather_fusion.1, pred[16]{0:T(512)(128)(4,1)S(1)} %and_reduce_fusion), kind=kLoop, calls=%fused_computation.11 | loop fusion | flops 1572864 | bytes 12582928 | tf_op jit(solution)/shard_map/jit(_take)/select_n | solution.py:42
  18.1 10.0 %all-to-all-start.1 = ((f32[16,32,3072]{2,1,0:T(8,128)}), f32[16,32,3072]{2,1,0:T(8,128)}, u32[]{:S(2)}, u32[]{:S(2)}) async-start(f32[16,32,3072]{2,1,0:T(8,128)} %broadcast_select_fusion), calls=%async_computation.1 | async-start | bytes 12582912 | tf_op jit(solution)/shard_map/all_to_all | solution.py:43
  28.2 5.0 %gather_fusion = f32[16,4,4,32,32]{4,3,2,1,0:T(8,128)} fusion(f32[4,16,4,32,32]{4,3,2,1,0:T(8,128)} %param.9, s32[1024]{0:T(1024)S(1)} %pad_clamp_fusion.1), kind=kCustom, calls=%fused_computation | custom fusion | bytes 2097216 | tf_op jit(solution)/shard_map/jit(_take)/gather | solution.py:46
  46.3 120.3 %all-to-all-done.1 = f32[16,32,3072]{2,1,0:T(8,128)} async-done(((f32[16,32,3072]{2,1,0:T(8,128)}), f32[16,32,3072]{2,1,0:T(8,128)}, u32[]{:S(2)}, u32[]{:S(2)}) %all-to-all-start.1) | async-done | bytes 6291488 | tf_op jit(solution)/shard_map/all_to_all | solution.py:43
  166.6 6.8 %all-to-all-start = ((f32[128,2,16,96]{3,2,1,0:T(8,128)}), f32[128,2,16,96]{3,2,1,0:T(8,128)S(1)}, u32[]{:S(2)}, u32[]{:S(2)}) async-start(f32[128,2,16,96]{3,2,1,0:T(8,128)} %copy.55), calls=%async_computation | async-start | bytes 4194304 | tf_op jit(solution)/shard_map/all_to_all | solution.py:71
  173.4 5.6 %convolution_multiply_fusion.3 = f32[128,3072]{1,0:T(8,128)S(1)} fusion(f32[128,512]{1,0:T(8,128)S(1)} %squeeze.23, f32[512,3072]{1,0:T(8,128)} %bitcast.8, f32[3072]{0:T(1024)S(1)} %broadcast_in_dim.51), kind=kOutput, calls=%fused_computation.10 | convolution fusion | flops 2416312320 | bytes 8138752 | tf_op jit(solution)/shard_map/dot_general | solution.py:56
  179.0 5.6 %fusion.3 = f32[128,3072]{1,0:T(8,128)S(1)} fusion(f32[128,3072]{1,0:T(8,128)S(1)} %convolution_multiply_fusion.3, f32[128,512]{1,0:T(8,128)S(1)} %squeeze.24, f32[512,3072]{1,0:T(8,128)} %bitcast.8, f32[3072]{0:T(1024)S(1)} %broadcast_in_dim.57), kind=kOutput, calls=%fused_computation.9 | convolution fusion | flops 2416705536 | bytes 9711616 | tf_op jit(solution)/shard_map/dot_general | solution.py:56
  184.6 5.6 %fusion.2 = f32[128,3072]{1,0:T(8,128)S(1)} fusion(f32[128,3072]{1,0:T(8,128)S(1)} %fusion.3, f32[128,512]{1,0:T(8,128)S(1)} %copy-done.6, f32[512,3072]{1,0:T(8,128)} %bitcast.8, f32[3072]{0:T(1024)S(1)} %broadcast_in_dim.59), kind=kOutput, calls=%fused_computation.7 | convolution fusion | flops 2416705536 | bytes 9711616 | tf_op jit(solution)/shard_map/dot_general | solution.py:56
  190.2 7.3 %fusion.1 = f32[128,3072]{1,0:T(8,128)} fusion(f32[128,3072]{1,0:T(8,128)S(1)} %fusion.2, f32[128,512]{1,0:T(8,128)S(1)} %copy-done.7, f32[512,3072]{1,0:T(8,128)} %bitcast.8, f32[3072]{0:T(1024)S(1)} %broadcast_in_dim.61), kind=kOutput, calls=%fused_computation.5 | convolution fusion | flops 2416705536 | bytes 9711616 | tf_op jit(solution)/shard_map/dot_general | solution.py:56
  197.6 3.0 copy.67
  200.6 3.0 copy.68
  204.9 6.7 %all-to-all-start.2 = ((f32[128,2,16,96]{3,2,1,0:T(8,128)}), f32[128,2,16,96]{3,2,1,0:T(8,128)}, u32[]{:S(2)}, u32[]{:S(2)}) async-start(f32[128,2,16,96]{3,2,1,0:T(8,128)} %copy.68), calls=%async_computation.2 | async-start | bytes 4194304 | tf_op jit(solution)/shard_map/all_to_all | solution.py:72
  211.7 2.8 copy.56
  224.8 2.8 fusion.4
  227.6 2.9 copy.61
  230.5 2.6 reshape.225
  233.1 2.7 multiply_reduce_fusion
  235.8 4.0 all-to-all-done.2
  239.8 4.1 %copy.69 = f32[8,2,16,16,96]{4,3,2,1,0:T(8,128)} copy(f32[8,2,16,16,96]{4,2,1,0,3:T(8,128)} %bitcast.14) | data formatting | bytes 3145728 | tf_op jit(solution)/shard_map/all_to_all | solution.py:72
  244.0 3.1 all_to_all.36
  250.3 77.7 %all-reduce.2 = (f32[]{:T(128)}, f32[]{:T(128)}, f32[]{:T(128)}) all-reduce(f32[]{:T(128)} %get-tuple-element.3, f32[]{:T(128)} %multiply_reduce_fusion, f32[]{:T(128)} %get-tuple-element.2), channel_id=1, replica_groups=mesh['chan'=16,'rad'=16] {'chan','rad'}, use_global_device_ids=true, to_apply=%region_5.6 | all-reduce | flops 3 | bytes 24 | tf_op jit(solution)/shard_map/psum | solution.py:83
  334.2 72.6 %psum.31 = f32[]{:T(128)} all-reduce(f32[]{:T(128)} %fusion.13), channel_id=1, replica_groups=mesh['chan'=16,'rad'=16] {'chan','rad'}, use_global_device_ids=true, to_apply=%region_7.8 | all-reduce | flops 1 | bytes 8 | tf_op jit(solution)/shard_map/psum | solution.py:89
  (66 shorter events, 39.0 us)
Async XLA Ops:
  0.6 224.2 %copy-start = (f32[12,128,128]{2,1,0:T(8,128)S(1)}, f32[12,128,128]{2,1,0:T(8,128)}, u32[]{:S(2)}) copy-start(f32[12,128,128]{2,1,0:T(8,128)} %param.14) | copy-start | bytes 2359300
  18.1 148.5 %all-to-all-start.1 = ((f32[16,32,3072]{2,1,0:T(8,128)}), f32[16,32,3072]{2,1,0:T(8,128)}, u32[]{:S(2)}, u32[]{:S(2)}) async-start(f32[16,32,3072]{2,1,0:T(8,128)} %broadcast_select_fusion), calls=%async_computation.1 | async-start | bytes 12582912 | tf_op jit(solution)/shard_map/all_to_all | solution.py:43
  28.2 5.0 %copy-start.8 = (s32[4]{0:T(128)S(1)}, s32[4]{0:T(128)}, u32[]{:S(2)}) copy-start(s32[4]{0:T(128)} %param.11) | copy-start | bytes 52
  37.8 1.1 copy-start.9
  37.8 1.1 copy-start.10
  166.6 37.0 %all-to-all-start = ((f32[128,2,16,96]{3,2,1,0:T(8,128)}), f32[128,2,16,96]{3,2,1,0:T(8,128)S(1)}, u32[]{:S(2)}, u32[]{:S(2)}) async-start(f32[128,2,16,96]{3,2,1,0:T(8,128)} %copy.55), calls=%async_computation | async-start | bytes 4194304 | tf_op jit(solution)/shard_map/all_to_all | solution.py:71
  179.0 5.6 %copy-start.6 = (f32[128,512]{1,0:T(8,128)S(1)}, f32[128,512]{1,0:T(8,128)}, u32[]{:S(2)}) copy-start(f32[128,512]{1,0:T(8,128)} %squeeze.25) | copy-start | bytes 786436
  184.6 5.6 %copy-start.7 = (f32[128,512]{1,0:T(8,128)S(1)}, f32[128,512]{1,0:T(8,128)}, u32[]{:S(2)}) copy-start(f32[128,512]{1,0:T(8,128)} %squeeze.26) | copy-start | bytes 786436
  203.6 1.3 copy-start.4
  204.9 34.9 %all-to-all-start.2 = ((f32[128,2,16,96]{3,2,1,0:T(8,128)}), f32[128,2,16,96]{3,2,1,0:T(8,128)}, u32[]{:S(2)}, u32[]{:S(2)}) async-start(f32[128,2,16,96]{3,2,1,0:T(8,128)} %copy.68), calls=%async_computation.2 | async-start | bytes 4194304 | tf_op jit(solution)/shard_map/all_to_all | solution.py:72
  214.4 1.4 copy-start.3
  219.7 2.2 copy-start.5
  249.1 1.1 copy-start.1
  330.5 2.4 copy-start.2
where the time goes:
time: 412 us; the launch traced here: 410 us
  blocking collectives  150 us (36%)
  waiting for transfers between devices  124 us (30%)
  local copies, waits for them, and re-layouts  54.6 us (13%)
  matrix products  29.7 us (7%)
  other arithmetic  23.9 us (6%)
  starting transfers between devices  23.5 us (6%)
  between operations  4.18 us (1%)
    all_to_all x1, waiting for transfers between devices, coupling_products(): lax.all_to_all(outgoing, 'chan', split_axis=0, concat_axis=0, tiled=True)  120 us
    psum x1, blocking collectives, per_device(): lax.psum((cross_re, cross_im, self_sq), ('chan', 'rad'))  77.7 us
    psum x1, blocking collectives, per_device(): lax.psum(jnp.sum(orth_re * orth_re + orth_im * orth_im), ('chan', 'rad'))  72.6 us
    dot_general x4, matrix products, coupling_products(): jnp.dot(matrices[order], incoming, precision=lax.Precision.HIGHEST, prefe...  24.1 us
    all_to_all x1, starting transfers between devices, coupling_products(): lax.all_to_all(outgoing, 'chan', split_axis=0, concat_axis=0, tiled=True)  9.98 us
  transfers between devices with their start and end apart: 3, of which 2 were waited for; matrix products, arithmetic and copies ran while one was open for 17% of the time, Pallas kernels for 0%

commit v1 on v0

--- a/solution.py
+++ b/solution.py
@@ -80,7 +80,7 @@
     cross_re = jnp.sum(state_re * wave_re + state_im * wave_im)
     cross_im = jnp.sum(state_re * wave_im - state_im * wave_re)
     self_sq = jnp.sum(state_here * state_here)
-    cross_re, cross_im, self_sq = lax.psum((cross_re, cross_im, self_sq), ("chan", "rad"))
+    cross_re, cross_im, self_sq = lax.psum(lax.psum((cross_re, cross_im, self_sq), "rad"), "chan")
     proj_re = cross_re / self_sq
     proj_im = cross_im / self_sq
     orth_re = wave_re - (proj_re * state_re - proj_im * state_im)

time: 412 us -> 398 us (0.966)
  blocking collectives: 150 us -> 136 us
    psum x1 -> x2, blocking collectives: 77.7 us -> 63.7 us  [the longest x1 33.3 us: per_device(): lax.psum(lax.psum((cross_re, cross_im, self_sq), 'rad'), 'chan')]
where the time goes in v1:
time: 398 us; the launch traced here: 397 us
  blocking collectives  136 us (34%)
  waiting for transfers between devices  124 us (31%)
  local copies, waits for them, and re-layouts  54.6 us (14%)
  matrix products  29.7 us (7%)
  other arithmetic  23.9 us (6%)
  starting transfers between devices  23.5 us (6%)
  between operations  4.17 us (1%)
    all_to_all x1, waiting for transfers between devices, coupling_products(): lax.all_to_all(outgoing, 'chan', split_axis=0, concat_axis=0, tiled=True)  120 us
    psum x1, blocking collectives, per_device(): lax.psum(jnp.sum(orth_re * orth_re + orth_im * orth_im), ('chan', 'rad'))  72.8 us
    psum x1, blocking collectives, per_device(): lax.psum(lax.psum((cross_re, cross_im, self_sq), 'rad'), 'chan')  33.3 us
    psum x1, blocking collectives, per_device(): lax.psum((cross_re, cross_im, self_sq), 'rad')  30.3 us
    dot_general x4, matrix products, coupling_products(): jnp.dot(matrices[order], incoming, precision=lax.Precision.HIGHEST, prefe...  24.1 us
    all_to_all x1, starting transfers between devices, coupling_products(): lax.all_to_all(outgoing, 'chan', split_axis=0, concat_axis=0, tiled=True)  9.98 us
  transfers between devices with their start and end apart: 3, of which 2 were waited for; matrix products, arithmetic and copies ran while one was open for 17% of the time, Pallas kernels for 0%

profile of v1, /device:TPU:1, one launch (start us, length us, event | category | flops | bytes accessed | tf_op | source)
XLA Modules:
  0.0 396.6 jit_solution(9500042594376296267)
XLA Ops:
  2.5 3.0 copy.55
  8.0 3.6 gather_fusion.1
  11.7 6.5 %broadcast_select_fusion = f32[16,32,3072]{2,1,0:T(8,128)} fusion(f32[16,32,3072]{2,1,0:T(8,128)} %gather_fusion.1, pred[16]{0:T(512)(128)(4,1)S(1)} %and_reduce_fusion), kind=kLoop, calls=%fused_computation.11 | loop fusion | flops 1572864 | bytes 12582928 | tf_op jit(solution)/shard_map/jit(_take)/select_n | solution.py:42
  18.1 10.0 %all-to-all-start.1 = ((f32[16,32,3072]{2,1,0:T(8,128)}), f32[16,32,3072]{2,1,0:T(8,128)}, u32[]{:S(2)}, u32[]{:S(2)}) async-start(f32[16,32,3072]{2,1,0:T(8,128)} %broadcast_select_fusion), calls=%async_computation.1 | async-start | bytes 12582912 | tf_op jit(solution)/shard_map/all_to_all | solution.py:43
  28.2 5.0 %gather_fusion = f32[16,4,4,32,32]{4,3,2,1,0:T(8,128)} fusion(f32[4,16,4,32,32]{4,3,2,1,0:T(8,128)} %param.9, s32[1024]{0:T(1024)S(1)} %pad_clamp_fusion.1), kind=kCustom, calls=%fused_computation | custom fusion | bytes 2097216 | tf_op jit(solution)/shard_map/jit(_take)/gather | solution.py:46
  46.3 120.3 %all-to-all-done.1 = f32[16,32,3072]{2,1,0:T(8,128)} async-done(((f32[16,32,3072]{2,1,0:T(8,128)}), f32[16,32,3072]{2,1,0:T(8,128)}, u32[]{:S(2)}, u32[]{:S(2)}) %all-to-all-start.1) | async-done | bytes 6291488 | tf_op jit(solution)/shard_map/all_to_all | solution.py:43
  166.6 6.8 %all-to-all-start = ((f32[128,2,16,96]{3,2,1,0:T(8,128)}), f32[128,2,16,96]{3,2,1,0:T(8,128)S(1)}, u32[]{:S(2)}, u32[]{:S(2)}) async-start(f32[128,2,16,96]{3,2,1,0:T(8,128)} %copy.55), calls=%async_computation | async-start | bytes 4194304 | tf_op jit(solution)/shard_map/all_to_all | solution.py:71
  173.4 5.6 %convolution_multiply_fusion.3 = f32[128,3072]{1,0:T(8,128)S(1)} fusion(f32[128,512]{1,0:T(8,128)S(1)} %squeeze.23, f32[512,3072]{1,0:T(8,128)} %bitcast.8, f32[3072]{0:T(1024)S(1)} %broadcast_in_dim.51), kind=kOutput, calls=%fused_computation.10 | convolution fusion | flops 2416312320 | bytes 8138752 | tf_op jit(solution)/shard_map/dot_general | solution.py:56
  179.0 5.6 %fusion.3 = f32[128,3072]{1,0:T(8,128)S(1)} fusion(f32[128,3072]{1,0:T(8,128)S(1)} %convolution_multiply_fusion.3, f32[128,512]{1,0:T(8,128)S(1)} %squeeze.24, f32[512,3072]{1,0:T(8,128)} %bitcast.8, f32[3072]{0:T(1024)S(1)} %broadcast_in_dim.57), kind=kOutput, calls=%fused_computation.9 | convolution fusion | flops 2416705536 | bytes 9711616 | tf_op jit(solution)/shard_map/dot_general | solution.py:56
  184.6 5.6 %fusion.2 = f32[128,3072]{1,0:T(8,128)S(1)} fusion(f32[128,3072]{1,0:T(8,128)S(1)} %fusion.3, f32[128,512]{1,0:T(8,128)S(1)} %copy-done.6, f32[512,3072]{1,0:T(8,128)} %bitcast.8, f32[3072]{0:T(1024)S(1)} %broadcast_in_dim.59), kind=kOutput, calls=%fused_computation.7 | convolution fusion | flops 2416705536 | bytes 9711616 | tf_op jit(solution)/shard_map/dot_general | solution.py:56
  190.2 7.3 %fusion.1 = f32[128,3072]{1,0:T(8,128)} fusion(f32[128,3072]{1,0:T(8,128)S(1)} %fusion.2, f32[128,512]{1,0:T(8,128)S(1)} %copy-done.7, f32[512,3072]{1,0:T(8,128)} %bitcast.8, f32[3072]{0:T(1024)S(1)} %broadcast_in_dim.61), kind=kOutput, calls=%fused_computation.5 | convolution fusion | flops 2416705536 | bytes 9711616 | tf_op jit(solution)/shard_map/dot_general | solution.py:56
  197.6 3.0 copy.67
  200.6 3.0 copy.68
  204.9 6.7 %all-to-all-start.2 = ((f32[128,2,16,96]{3,2,1,0:T(8,128)}), f32[128,2,16,96]{3,2,1,0:T(8,128)}, u32[]{:S(2)}, u32[]{:S(2)}) async-start(f32[128,2,16,96]{3,2,1,0:T(8,128)} %copy.68), calls=%async_computation.2 | async-start | bytes 4194304 | tf_op jit(solution)/shard_map/all_to_all | solution.py:72
  211.7 2.8 copy.56
  224.8 2.8 fusion.4
  227.6 2.9 copy.61
  233.1 2.7 multiply_reduce_fusion
  235.8 4.0 %all-to-all-done.2 = f32[128,2,16,96]{3,2,1,0:T(8,128)} async-done(((f32[128,2,16,96]{3,2,1,0:T(8,128)}), f32[128,2,16,96]{3,2,1,0:T(8,128)}, u32[]{:S(2)}, u32[]{:S(2)}) %all-to-all-start.2) | async-done | bytes 1572896 | tf_op jit(solution)/shard_map/all_to_all | solution.py:72
  239.8 4.1 %copy.69 = f32[8,2,16,16,96]{4,3,2,1,0:T(8,128)} copy(f32[8,2,16,16,96]{4,2,1,0,3:T(8,128)} %bitcast.14) | data formatting | bytes 3145728 | tf_op jit(solution)/shard_map/all_to_all | solution.py:72
  244.0 3.1 all_to_all.36
  250.3 30.3 %all-reduce.2 = (f32[]{:T(128)}, f32[]{:T(128)}, f32[]{:T(128)}) all-reduce(f32[]{:T(128)} %get-tuple-element.3, f32[]{:T(128)} %multiply_reduce_fusion, f32[]{:T(128)} %get-tuple-element.2), channel_id=1, replica_groups=mesh['chan'=16,'rad'=16] {'rad'}, use_global_device_ids=true, to_apply=%region_7.8 | all-reduce | flops 3 | bytes 24 | tf_op jit(solution)/shard_map/psum | solution.py:83
  280.6 33.3 %all-reduce.3 = (f32[]{:T(128)}, f32[]{:T(128)}, f32[]{:T(128)}) all-reduce(f32[]{:T(128)} %get-tuple-element.4, f32[]{:T(128)} %get-tuple-element.5, f32[]{:T(128)} %get-tuple-element.6), channel_id=1, replica_groups=mesh['chan'=16,'rad'=16] {'chan'}, use_global_device_ids=true, to_apply=%region_8.9 | all-reduce | flops 3 | bytes 24 | tf_op jit(solution)/shard_map/psum | solution.py:83
  320.1 72.8 %psum.55 = f32[]{:T(128)} all-reduce(f32[]{:T(128)} %fusion.13), channel_id=1, replica_groups=mesh['chan'=16,'rad'=16] {'chan','rad'}, use_global_device_ids=true, to_apply=%region_10.11 | all-reduce | flops 1 | bytes 8 | tf_op jit(solution)/shard_map/psum | solution.py:89
  (67 shorter events, 41.6 us)
Async XLA Ops:
  0.6 224.2 %copy-start = (f32[12,128,128]{2,1,0:T(8,128)S(1)}, f32[12,128,128]{2,1,0:T(8,128)}, u32[]{:S(2)}) copy-start(f32[12,128,128]{2,1,0:T(8,128)} %param.14) | copy-start | bytes 2359300
  18.1 148.5 %all-to-all-start.1 = ((f32[16,32,3072]{2,1,0:T(8,128)}), f32[16,32,3072]{2,1,0:T(8,128)}, u32[]{:S(2)}, u32[]{:S(2)}) async-start(f32[16,32,3072]{2,1,0:T(8,128)} %broadcast_select_fusion), calls=%async_computation.1 | async-start | bytes 12582912 | tf_op jit(solution)/shard_map/all_to_all | solution.py:43
  28.2 5.0 %copy-start.8 = (s32[4]{0:T(128)S(1)}, s32[4]{0:T(128)}, u32[]{:S(2)}) copy-start(s32[4]{0:T(128)} %param.11) | copy-start | bytes 52
  37.8 1.1 copy-start.9
  37.8 1.1 copy-start.10
  166.6 37.0 %all-to-all-start = ((f32[128,2,16,96]{3,2,1,0:T(8,128)}), f32[128,2,16,96]{3,2,1,0:T(8,128)S(1)}, u32[]{:S(2)}, u32[]{:S(2)}) async-start(f32[128,2,16,96]{3,2,1,0:T(8,128)} %copy.55), calls=%async_computation | async-start | bytes 4194304 | tf_op jit(solution)/shard_map/all_to_all | solution.py:71
  179.0 5.6 %copy-start.6 = (f32[128,512]{1,0:T(8,128)S(1)}, f32[128,512]{1,0:T(8,128)}, u32[]{:S(2)}) copy-start(f32[128,512]{1,0:T(8,128)} %squeeze.25) | copy-start | bytes 786436
  184.6 5.6 %copy-start.7 = (f32[128,512]{1,0:T(8,128)S(1)}, f32[128,512]{1,0:T(8,128)}, u32[]{:S(2)}) copy-start(f32[128,512]{1,0:T(8,128)} %squeeze.26) | copy-start | bytes 786436
  203.6 1.3 copy-start.4
  204.9 34.9 %all-to-all-start.2 = ((f32[128,2,16,96]{3,2,1,0:T(8,128)}), f32[128,2,16,96]{3,2,1,0:T(8,128)}, u32[]{:S(2)}, u32[]{:S(2)}) async-start(f32[128,2,16,96]{3,2,1,0:T(8,128)} %copy.68), calls=%async_computation.2 | async-start | bytes 4194304 | tf_op jit(solution)/shard_map/all_to_all | solution.py:72
  214.4 1.4 copy-start.3
  219.7 2.2 copy-start.5
  249.1 1.1 copy-start.1
  316.5 2.4 copy-start.2
